TPU v7x, 128 devices: a whole 4x4x4 slice. The times are simulated.
128 devices in a mesh: dp: 8 (over z_lo, x), mp: 16 (over z_hi, y, core).
Axes of the slice: x: 4, y: 4, z: 4 (z_hi: 2, z_lo: 2; z = z_hi * 2 + z_lo), core: 2. Of those that a mesh axis runs over, the one named last changes fastest.
Arguments:
- inputs: bfloat16 [256, 256, 3072], P('mp', None, 'dp'), may hold values from -6 to 6
- hidden_pre: bfloat16 [256, 256, 3072], P('mp', None, 'dp'), may hold values from -8 to 8
- cotangent: bfloat16 [256, 256, 3072], P('mp', None, 'dp'), may hold values from -6 to 6
- r1_weight: bfloat16 [256, 256, 256], P('mp'), may hold values from -0.375 to 0.375
- l1_weight: bfloat16 [256, 256, 256], P('mp'), may hold values from -0.375 to 0.375
- r2_weight: bfloat16 [256, 256, 256], P('mp'), may hold values from -0.375 to 0.375
- l2_weight: bfloat16 [256, 256, 256], P('mp'), may hold values from -0.375 to 0.375
Outputs:
- grad_inputs: bfloat16 [256, 256, 3072], P('mp', None, 'dp')
- grad_r1: float32 [256, 256, 256], P('mp', 'dp')
- grad_l1: float32 [256, 256, 256], P('mp', 'dp')
- grad_r2: float32 [256, 256, 256], P('mp', 'dp')
- grad_l2: float32 [256, 256, 256], P('mp', 'dp')
All inputs are finite; a program needn't handle non-finite values.
Results may differ from a plain program's by a relative error of at most 0.008.
Values may be sent and summed in bfloat16 or wider, within the bound.
A program may use at most 128 MiB of HBM per device.

v0:
```python
import jax
import jax.numpy as jnp
from jax import lax
from jax.sharding import PartitionSpec as P


def gelu_pair(value):
    coeff = 0.7978845608
    inner = coeff * (value + 0.044715 * value * value * value)
    tangent = jnp.tanh(inner)
    result = 0.5 * value * (1.0 + tangent)
    slope = 0.5 * (1.0 + tangent) + 0.5 * value * (1.0 - tangent * tangent) * coeff * (
        1.0 + 3.0 * 0.044715 * value * value
    )
    return (result, slope)


def contract(form, left, right):
    return jnp.einsum(form, left, right, preferred_element_type=jnp.float32)


def body(inputs, hidden_pre, cotangent, r1_weight, l1_weight, r2_weight, l2_weight):
    r1_out = contract("bio,bit->bot", r1_weight, inputs).astype(jnp.bfloat16)
    l1_input = lax.all_to_all(r1_out, "mp", split_axis=1, concat_axis=0, tiled=True)
    act_val, slope = gelu_pair(hidden_pre.astype(jnp.float32))
    act = act_val.astype(jnp.bfloat16)
    r2_out = contract("oqr,oqt->ort", r2_weight, act).astype(jnp.bfloat16)
    l2_input = lax.all_to_all(r2_out, "mp", split_axis=1, concat_axis=0, tiled=True)
    d_l2in = contract("ros,rst->rot", l2_weight, cotangent).astype(jnp.bfloat16)
    term_l2 = contract("ort,rst->ros", l2_input, cotangent)
    d_r2out = lax.all_to_all(d_l2in, "mp", split_axis=1, concat_axis=0, tiled=True)
    term_r2 = contract("oqt,rot->oqr", act, d_r2out)
    d_hidden = (contract("oqr,rot->oqt", r2_weight, d_r2out) * slope).astype(jnp.bfloat16)
    term_l1 = contract("bot,oqt->obq", l1_input, d_hidden)
    d_l1in = contract("obq,oqt->obt", l1_weight, d_hidden).astype(jnp.bfloat16)
    d_r1out = lax.all_to_all(d_l1in, "mp", split_axis=1, concat_axis=0, tiled=True)
    term_r1 = contract("bit,obt->bio", inputs, d_r1out)
    grad_r1, grad_l1, grad_r2, grad_l2 = (
        lax.psum_scatter(
            term_r1.astype(jnp.bfloat16), "dp", scatter_dimension=1, tiled=True
        ).astype(jnp.float32),
        lax.psum_scatter(
            term_l1.astype(jnp.bfloat16), "dp", scatter_dimension=1, tiled=True
        ).astype(jnp.float32),
        lax.psum_scatter(
            term_r2.astype(jnp.bfloat16), "dp", scatter_dimension=1, tiled=True
        ).astype(jnp.float32),
        lax.psum_scatter(
            term_l2.astype(jnp.bfloat16), "dp", scatter_dimension=1, tiled=True
        ).astype(jnp.float32),
    )
    grad_inputs = contract("bio,obt->bit", r1_weight, d_r1out).astype(jnp.bfloat16)
    return (grad_inputs, grad_r1, grad_l1, grad_r2, grad_l2)


def solution(mesh):
    placed = (
        P("mp", None, "dp"),
        P("mp", None, "dp"),
        P("mp", None, "dp"),
        P("mp", None, None),
        P("mp", None, None),
        P("mp", None, None),
        P("mp", None, None),
    )
    return jax.shard_map(
        body,
        mesh=mesh,
        in_specs=placed,
        out_specs=(
            P("mp", None, "dp"),
            P("mp", "dp", None),
            P("mp", "dp", None),
            P("mp", "dp", None),
            P("mp", "dp", None),
        ),
        check_vma=False,
    )
```

profile of v0, /device:TPU:0, one launch (start us, length us, event | category | flops | bytes accessed | tf_op | source)
XLA Modules:
  0.0 340.8 jit_solution(9344195628247134512)
XLA Ops:
  7.2 4.8 %copy.64 = bf16[16,256,384]{1,2,0:T(8,128)(2,1)} copy(bf16[16,256,384]{2,1,0:T(8,128)(2,1)} %param.8) | data formatting | bytes 6291456 | tf_op args[1]
  12.0 6.5 %convert_bitcast_fusion = bf16[16,256,384]{1,2,0:T(8,128)(2,1)} fusion(bf16[16,256,256]{2,1,0:T(8,128)(2,1)} %param.12, bf16[16,256,384]{1,2,0:T(8,128)(2,1)} %copy.64), kind=kOutput, calls=%fused_computation.18 | convolution fusion | flops 822607872 | bytes 8388608 | tf_op jit(solution)/shard_map/oqr,oqt->ort/dot_general | solution.py:19
  18.6 5.1 %copy.77 = bf16[16,256,384]{2,0,1:T(8,128)(2,1)} copy(bf16[16,256,384]{1,2,0:T(8,128)(2,1)} %convert_bitcast_fusion) | data formatting | bytes 6291456 | tf_op jit(solution)/shard_map/convert_element_type | solution.py:27
  23.7 48.4 %all_to_all.72 = bf16[16,256,384]{2,0,1:T(8,128)(2,1)S(1)} all-to-all(bf16[16,256,384]{2,0,1:T(8,128)(2,1)} %copy.77), channel_id=1, replica_groups=mesh['dp'=8,'mp'=16] {'mp'}, dimensions={1} | all-to-all | bytes 6291456 | tf_op jit(solution)/shard_map/all_to_all | solution.py:28
  72.6 2.7 convolution_convert_fusion.2
  75.2 2.8 convolution_convert_fusion.1
  78.1 3.6 %copy.60 = bf16[16,256,384]{2,0,1:T(8,128)(2,1)} copy(bf16[16,256,384]{2,1,0:T(8,128)(2,1)S(1)} %convolution_convert_fusion.1) | data formatting | bytes 6291456 | tf_op jit(solution)/shard_map/convert_element_type | solution.py:29
  81.7 3.7 %all-to-all-start = ((bf16[16,256,384]{2,0,1:T(8,128)(2,1)}), bf16[16,256,384]{2,0,1:T(8,128)(2,1)S(1)}, u32[]{:S(2)}, u32[]{:S(2)}) async-start(bf16[16,256,384]{2,0,1:T(8,128)(2,1)} %copy.60), calls=%async_computation | async-start | bytes 6291456 | tf_op jit(solution)/shard_map/all_to_all | solution.py:31
  85.4 3.8 %convolution_convert_fusion = bf16[16,256,384]{2,1,0:T(8,128)(2,1)S(1)} fusion(bf16[16,256,256]{2,1,0:T(8,128)(2,1)} %param.10, bf16[16,256,384]{2,1,0:T(8,128)(2,1)} %param.7), kind=kOutput, calls=%fused_computation.29 | convolution fusion | flops 806879232 | bytes 8388608 | tf_op jit(solution)/shard_map/bio,bit->bot/dot_general | solution.py:19
  89.3 3.5 %copy.72 = bf16[16,256,384]{2,0,1:T(8,128)(2,1)} copy(bf16[16,256,384]{2,1,0:T(8,128)(2,1)S(1)} %convolution_convert_fusion) | data formatting | bytes 6291456 | tf_op jit(solution)/shard_map/convert_element_type | solution.py:23
  92.8 47.1 %all-to-all-done = bf16[16,256,384]{2,0,1:T(8,128)(2,1)S(1)} async-done(((bf16[16,256,384]{2,0,1:T(8,128)(2,1)}), bf16[16,256,384]{2,0,1:T(8,128)(2,1)S(1)}, u32[]{:S(2)}, u32[]{:S(2)}) %all-to-all-start) | async-done | bytes 3145760 | tf_op jit(solution)/shard_map/all_to_all | solution.py:31
  141.7 4.4 %all-to-all-start.2 = ((bf16[16,256,384]{2,0,1:T(8,128)(2,1)}), bf16[16,256,384]{2,0,1:T(8,128)(2,1)S(1)}, u32[]{:S(2)}, u32[]{:S(2)}) async-start(bf16[16,256,384]{2,0,1:T(8,128)(2,1)} %copy.72), calls=%async_computation.3 | async-start | bytes 6291456 | tf_op jit(solution)/shard_map/all_to_all | solution.py:24
  146.2 2.8 copy.62
  150.8 4.4 %fusion.25 = bf16[16,256,256]{2,1,0:T(8,128)(2,1)} fusion(bf16[256,16,384]{2,1,0:T(8,128)(2,1)S(1)} %bitcast.48, bf16[16,256,384]{1,2,0:T(8,128)(2,1)S(1)} %copy-done.3), kind=kOutput, calls=%fused_computation.32 | convolution fusion | flops 822083584 | bytes 8388608 | tf_op jit(solution)/shard_map/oqt,rot->oqr/dot_general | solution.py:19
  155.4 42.8 %all-to-all-done.2 = bf16[16,256,384]{2,0,1:T(8,128)(2,1)S(1)} async-done(((bf16[16,256,384]{2,0,1:T(8,128)(2,1)}), bf16[16,256,384]{2,0,1:T(8,128)(2,1)S(1)}, u32[]{:S(2)}, u32[]{:S(2)}) %all-to-all-start.2) | async-done | bytes 3145760 | tf_op jit(solution)/shard_map/all_to_all | solution.py:24
  201.0 7.0 %fusion.6 = bf16[16,256,384]{1,2,0:T(8,128)(2,1)S(1)} fusion(bf16[16,256,384]{1,2,0:T(8,128)(2,1)S(1)} %copy-done.4, bf16[16,256,256]{2,1,0:T(8,128)(2,1)} %param.12, bf16[256,16,384]{2,1,0:T(8,128)(2,1)S(1)} %bitcast.49), kind=kOutput, calls=%fused_computation.13 | convolution fusion | flops 836763648 | bytes 11534336 | tf_op jit(solution)/shard_map/oqr,rot->oqt/dot_general | solution.py:19
  208.0 2.7 convolution_convert_fusion.3
  210.8 4.3 %convert_bitcast_fusion.2 = bf16[16,256,384]{1,2,0:T(8,128)(2,1)} fusion(bf16[16,256,384]{1,2,0:T(8,128)(2,1)S(1)} %fusion.6, bf16[16,256,256]{2,1,0:T(8,128)(2,1)} %param.11), kind=kOutput, calls=%fused_computation.20 | convolution fusion | flops 806879232 | bytes 8388608 | tf_op jit(solution)/shard_map/obq,oqt->obt/dot_general | solution.py:19
  215.1 3.9 %copy.65 = bf16[16,256,384]{2,0,1:T(8,128)(2,1)S(1)} copy(bf16[16,256,384]{1,2,0:T(8,128)(2,1)} %convert_bitcast_fusion.2) | data formatting | bytes 6291456 | tf_op jit(solution)/shard_map/convert_element_type | solution.py:35
  218.9 62.6 %all_to_all.73 = bf16[16,256,384]{2,0,1:T(8,128)(2,1)S(1)} all-to-all(bf16[16,256,384]{2,0,1:T(8,128)(2,1)S(1)} %copy.65), channel_id=1, replica_groups=mesh['dp'=8,'mp'=16] {'mp'}, dimensions={1} | all-to-all | bytes 6291456 | tf_op jit(solution)/shard_map/all_to_all | solution.py:36
  286.1 4.5 %copy.70 = bf16[16,256,256]{2,0,1:T(8,128)(2,1)} copy(bf16[16,256,256]{1,2,0:T(8,128)(2,1)} %convert_bitcast_fusion.3) | data formatting | bytes 4194304 | tf_op jit(solution)/shard_map/convert_element_type | solution.py:40
  290.6 4.7 %convert_bitcast_fusion.1 = bf16[16,256,384]{1,2,0:T(8,128)(2,1)} fusion(bf16[16,256,256]{2,1,0:T(8,128)(2,1)} %param.10, bf16[256,16,384]{2,1,0:T(8,128)(2,1)S(1)} %bitcast.45), kind=kOutput, calls=%fused_computation.19 | convolution fusion | flops 806879232 | bytes 8388608 | tf_op jit(solution)/shard_map/bio,obt->bit/dot_general | solution.py:19
  295.3 4.8 %copy.80 = bf16[16,256,384]{2,1,0:T(8,128)(2,1)} copy(bf16[16,256,384]{1,2,0:T(8,128)(2,1)} %convert_bitcast_fusion.1) | data formatting | bytes 6291456
  305.5 26.9 %reduce-scatter.5.cloned.1.call-done = bf16[16,32,256]{2,0,1:T(8,128)(2,1)} async-done(((bf16[16,256,256]{2,0,1:T(8,128)(2,1)}), bf16[16,32,256]{2,0,1:T(8,128)(2,1)}) %reduce-scatter.5.cloned.1.call-update) | async-done | bytes 262160 | tf_op jit(solution)/shard_map/reduce_scatter | solution.py:39
  (35 shorter events, 18.8 us)
Async XLA Ops:
  7.2 65.4 %copy-start = (bf16[16,256,384]{2,1,0:T(8,128)(2,1)S(1)}, bf16[16,256,384]{2,1,0:T(8,128)(2,1)}, u32[]{:S(2)}) copy-start(bf16[16,256,384]{2,1,0:T(8,128)(2,1)} %param.9) | copy-start | bytes 9437188
  7.2 292.9 %reduce-scatter.11.cloned.1.call-start = ((), (), s32[]{:S(2)}) async-start(), calls=%async_computation.11 | async-start | bytes 2359296 | tf_op jit(solution)/shard_map/reduce_scatter | solution.py:48
  81.7 58.3 %all-to-all-start = ((bf16[16,256,384]{2,0,1:T(8,128)(2,1)}), bf16[16,256,384]{2,0,1:T(8,128)(2,1)S(1)}, u32[]{:S(2)}, u32[]{:S(2)}) async-start(bf16[16,256,384]{2,0,1:T(8,128)(2,1)} %copy.60), calls=%async_computation | async-start | bytes 6291456 | tf_op jit(solution)/shard_map/all_to_all | solution.py:31
  140.0 1.8 copy-start.2
  141.7 56.4 %all-to-all-start.2 = ((bf16[16,256,384]{2,0,1:T(8,128)(2,1)}), bf16[16,256,384]{2,0,1:T(8,128)(2,1)S(1)}, u32[]{:S(2)}, u32[]{:S(2)}) async-start(bf16[16,256,384]{2,0,1:T(8,128)(2,1)} %copy.72), calls=%async_computation.3 | async-start | bytes 6291456 | tf_op jit(solution)/shard_map/all_to_all | solution.py:24
  146.2 155.7 %reduce-scatter.9.cloned.1.call-start = ((), (), s32[]{:S(2)}) async-start(), calls=%async_computation.10 | async-start | bytes 2359296 | tf_op jit(solution)/shard_map/reduce_scatter | solution.py:45
  146.2 4.6 %copy-start.3 = (bf16[16,256,384]{1,2,0:T(8,128)(2,1)S(1)}, bf16[16,256,384]{1,2,0:T(8,128)(2,1)}, u32[]{:S(2)}) copy-start(bf16[16,256,384]{1,2,0:T(8,128)(2,1)} %copy.64) | copy-start | bytes 9437188
  149.1 1.8 copy-start.5
  155.3 148.4 %reduce-scatter.7.cloned.1.call-start = ((), (), s32[]{:S(2)}) async-start(), calls=%async_computation.9 | async-start | bytes 2359296 | tf_op jit(solution)/shard_map/reduce_scatter | solution.py:42
  198.2 1.9 copy-start.4
  198.2 2.9 copy-start.6
  210.7 121.7 %reduce-scatter.5.cloned.1.call-start = ((), (), s32[]{:S(2)}) async-start(), calls=%async_computation.8 | async-start | bytes 2359296 | tf_op jit(solution)/shard_map/reduce_scatter | solution.py:39
  281.6 1.9 copy-start.7
  295.3 38.9 %copy-start.1 = (bf16[16,256,384]{2,1,0:T(8,128)(2,1)S(1)}, bf16[16,256,384]{2,1,0:T(8,128)(2,1)}, u32[]{:S(2)}) copy-start(bf16[16,256,384]{2,1,0:T(8,128)(2,1)} %param.9) | copy-start | bytes 9437188
Sparse Core Ops, SparseCore 0:
  75.4 53.3 reduce-scatter.10
  155.4 53.0 reduce-scatter.8
  210.9 61.5 reduce-scatter.6
  290.8 41.5 reduce-scatter.4
where the time goes:
time: 342 us; the launch traced here: 341 us
  waiting for transfers between devices  117 us (34%)
  blocking collectives  111 us (32%)
  local copies, waits for them, and re-layouts  43.6 us (13%)
  matrix products  41.5 us (12%)
  between operations  13.9 us (4%)
  starting transfers between devices  8.35 us (2%)
  other arithmetic  5.37 us (2%)
    all_to_all x1, blocking collectives, body(): lax.all_to_all(d_l1in, 'mp', split_axis=1, concat_axis=0, tiled=True)  62.6 us
    all_to_all x1, blocking collectives, body(): lax.all_to_all(r2_out, 'mp', split_axis=1, concat_axis=0, tiled=True)  48.4 us
    all_to_all x1, waiting for transfers between devices, body(): lax.all_to_all(d_l2in, 'mp', split_axis=1, concat_axis=0, tiled=True)  47.1 us
    all_to_all x1, waiting for transfers between devices, body(): lax.all_to_all(r1_out, 'mp', split_axis=1, concat_axis=0, tiled=True)  42.8 us
    dot_general x10, matrix products, contract(): return jnp.einsum(form, left, right, preferred_element_type=jnp.float32)  41.5 us
    reduce_scatter x1, waiting for transfers between devices, body(): lax.psum_scatter(term_r1.astype(jnp.bfloat16), 'dp', scatter_dimension=1,...  26.9 us
    unnamed x19, local copies, waits for them, and re-layouts  18.4 us
  transfers between devices with their start and end apart: 6, of which 3 were waited for; matrix products, arithmetic and copies ran while one was open for 18% of the time, Pallas kernels for 0%

commit v1 on v0

v1 whole, which is shorter than its diff:
```python
import jax
import jax.numpy as jnp
from jax import lax
from jax.experimental import pallas as pl
from jax.experimental.pallas import tpu as pltpu
from jax.sharding import PartitionSpec as P

BF = jnp.bfloat16
F32 = jnp.float32
MESH = pl.DeviceIdType.MESH
NB, B, T = 16, 256, 384
CH = 4
NCH = NB // CH
LANES = 128
COEFF = 0.7978845608
D_L2IN, R1_OUT, D_L1IN, R2_OUT = range(4)
G_R2, G_L1, G_R1, G_L2 = range(4)


def dot(left, right, l_dim, r_dim):
    return lax.dot_general(
        left, right, (((l_dim,), (r_dim,)), ((), ())), preferred_element_type=F32
    )


def loop(count, step):
    lax.fori_loop(0, count, lambda i, carry: (step(i), carry)[1], 0)


def kernel(
    inp_h, hid_h, cot_h, r1_h, l1_h, r2_h, l2_h,
    ginp_h, gr1_h, gl1_h, gr2_h, gl2_h,
    inp, hid, cot, r1w, l1w, r2w, l2w,
    act, send, arrive, recv, part, xin, zout, zin, total, stage, prod,
    load_sem, out_sem, zs, zr, yo, yf, yr, xs, xr, ls, lr,
):
    d, m = lax.axis_index("dp"), lax.axis_index("mp")
    x, zl = d % 4, d // 4
    zh, yc = m // 8, m % 8
    y, core = yc // 2, yc % 2
    z_mate = (d, (1 - zh) * 8 + yc)
    l_mate = ((1 - zl) * 4 + x, m)
    near = []
    for dy, dc in ((2, 0), (2, 1), (1, 0), (3, 0), (1, 1), (3, 1), (0, 1)):
        near.append(((y + dy) % 4) * 2 + (core + dc) % 2)
    x_mates = [(zl * 4 + (x + dx) % 4, m) for dx in (1, 2, 3)]
    mate_m = (1 - zh) * 8 + yc

    loads = [
        pltpu.make_async_copy(src, dst, load_sem.at[i])
        for i, (src, dst) in enumerate(
            ((l2_h, l2w), (cot_h, cot), (r1_h, r1w), (inp_h, inp), (hid_h, hid), (r2_h, r2w), (l1_h, l1w))
        )
    ]
    for load in loads:
        load.start()

    barrier = pltpu.get_barrier_semaphore()
    mates = [z_mate, l_mate] + [(d, zh * 8 + n) for n in near] + x_mates
    for mate in mates:
        pl.semaphore_signal(barrier, inc=1, device_id=mate, device_id_type=MESH)

    def rows(c):
        return pl.ds(c * CH, CH)

    def remote(src, dst, s_sem, r_sem, device):
        return pltpu.make_async_remote_copy(
            src_ref=src, dst_ref=dst, send_sem=s_sem, recv_sem=r_sem, device_id=device, device_id_type=MESH
        )

    def await_bytes(ref, sem):
        pltpu.make_async_copy(ref, ref, sem).wait()

    def z_send(k, c):
        remote(
            send.at[k % 2, pl.ds((1 - zh) * 8, 8), rows(c)], arrive.at[k, :, rows(c)],
            zs.at[k, c], zr.at[k, c], z_mate,
        ).start()

    def y_own(k, c):
        for n in near:
            remote(
                send.at[k % 2, zh * 8 + n, rows(c)], recv.at[k, rows(c), m],
                yo.at[k, c], yr.at[k, c], (d, zh * 8 + n),
            ).start()
        pltpu.make_async_copy(send.at[k % 2, m, rows(c)], recv.at[k, rows(c), m], yr.at[k, c]).start()

    def y_forward(k, c):
        await_bytes(arrive.at[k, :, rows(c)], zr.at[k, c])
        for n in near:
            remote(
                arrive.at[k, n, rows(c)], recv.at[k, rows(c), mate_m],
                yf.at[k, c], yr.at[k, c], (d, zh * 8 + n),
            ).start()
        pltpu.make_async_copy(arrive.at[k, yc, rows(c)], recv.at[k, rows(c), mate_m], yr.at[k, c]).start()

    def arrived(k, c):
        await_bytes(recv.at[k, rows(c)], yr.at[k, c])

    def sends_done(k, c):
        await_bytes(arrive.at[k, :, rows(c)], zs.at[k, c])
        await_bytes(arrive.at[k, pl.ds(0, 7), rows(c)], yo.at[k, c])
        await_bytes(arrive.at[k, pl.ds(0, 7), rows(c)], yf.at[k, c])

    def produce(k, weight, w_dim, data):
        def span(tc):
            lanes = pl.ds(pl.multiple_of(tc * LANES, LANES), LANES)

            def block(j):
                stage[pl.ds(j, B, stride=NB), :] = dot(weight[j], data[j, :, lanes], w_dim, 0)

            def pack(dest):
                rows_of = pl.ds(pl.multiple_of(dest * B, B), B)
                send[k % 2, dest, :, :, lanes] = stage[rows_of, :].astype(BF).reshape(NB, NB, LANES)

            loop(NB, block)
            loop(NB, pack)

        loop(T // LANES, span)

    def received(k, j):
        return recv[k, j].reshape(B, T)

    def gradient(g, j, value):
        part[g % 2, j] = value.astype(BF).reshape(2, 4, 32, B)

    def x_send(g, c):
        for i, mate in enumerate(x_mates):
            remote(
                part.at[g % 2, rows(c), :, (x + i + 1) % 4], xin.at[g, i, rows(c)],
                xs.at[g, c], xr.at[g, c], mate,
            ).start()

    def x_done(g, c):
        await_bytes(xin.at[g, :, rows(c)], xs.at[g, c])

    def x_sum(g, c):
        await_bytes(xin.at[g, :, rows(c)], xr.at[g, c])

        def block(i):
            j = c * CH + i

            def joined(half):
                value = part[g % 2, j, half, x].astype(F32)
                for s in range(3):
                    value += xin[g, s, j, half].astype(F32)
                return value

            zout[g, j] = joined(1 - zl).astype(BF)
            total[g, j] = joined(zl)

        loop(CH, block)
        remote(zout.at[g, rows(c)], zin.at[g, rows(c)], ls.at[g, c], lr.at[g, c], l_mate).start()

    grads_h = {G_R2: gr2_h, G_L1: gl1_h, G_R1: gr1_h, G_L2: gl2_h}

    def finish(g, c):
        await_bytes(zin.at[g, rows(c)], lr.at[g, c])

        def block(i):
            j = c * CH + i
            total[g, j] += zin[g, j].astype(F32)

        loop(CH, block)
        pltpu.make_async_copy(total.at[g, rows(c)], grads_h[g].at[rows(c)], out_sem.at[g, c]).start()

    def gelu_block(j):
        def group(i):
            span = pl.ds(pl.multiple_of(i * 32, 32), 32)
            v = hid[j, span, :].astype(F32)
            t = jnp.tanh(COEFF * (v + 0.044715 * v * v * v))
            act[j, span, :] = (0.5 * v * (1.0 + t)).astype(BF)

        loop(B // 32, group)

    def d_hidden_block(j):
        prod[...] = dot(r2w[j], received(D_L2IN, j), 1, 0)

        def group(i):
            span = pl.ds(pl.multiple_of(i * 32, 32), 32)
            v = hid[j, span, :].astype(F32)
            t = jnp.tanh(COEFF * (v + 0.044715 * v * v * v))
            slope = 0.5 * (1.0 + t) + 0.5 * v * (1.0 - t * t) * COEFF * (1.0 + 3.0 * 0.044715 * v * v)
            hid[j, span, :] = (prod[span, :] * slope).astype(BF)

        loop(B // 32, group)

    def each(c, step):
        loop(CH, lambda i: step(c * CH + i))

    loads[0].wait()
    loads[1].wait()
    produce(D_L2IN, l2w, 1, cot)
    pl.semaphore_wait(barrier, len(mates))
    loop(NCH, lambda c: z_send(D_L2IN, c))
    loop(NCH, lambda c: y_own(D_L2IN, c))
    loads[2].wait()
    loads[3].wait()
    produce(R1_OUT, r1w, 0, inp)
    loads[4].wait()

    def step(c):
        y_forward(D_L2IN, c)
        z_send(R1_OUT, c)
        y_own(R1_OUT, c)
        each(c, gelu_block)

    loop(NCH, step)
    loads[5].wait()

    def step(c):
        arrived(D_L2IN, c)
        each(c, d_hidden_block)
        each(c, lambda j: gradient(G_R2, j, dot(act[j], received(D_L2IN, j), 1, 1)))
        x_send(G_R2, c)

    loop(NCH, step)
    loads[6].wait()
    loop(NCH, lambda c: sends_done(D_L2IN, c))
    produce(D_L1IN, l1w, 1, hid)

    def step(c):
        y_forward(R1_OUT, c)
        z_send(D_L1IN, c)
        y_own(D_L1IN, c)
        x_sum(G_R2, c)

    loop(NCH, step)
    def step(c):
        arrived(R1_OUT, c)
        each(c, lambda j: gradient(G_L1, j, dot(received(R1_OUT, j), hid[j], 1, 1)))
        x_send(G_L1, c)

    loop(NCH, step)
    loop(NCH, lambda c: sends_done(R1_OUT, c))
    produce(R2_OUT, r2w, 0, act)

    def step(c):
        y_forward(D_L1IN, c)
        z_send(R2_OUT, c)
        y_own(R2_OUT, c)
        finish(G_R2, c)
        x_sum(G_L1, c)
        x_done(G_R2, c)

    loop(NCH, step)
    def step(c):
        arrived(D_L1IN, c)
        each(c, lambda j: gradient(G_R1, j, dot(inp[j], received(D_L1IN, j), 1, 1)))
        x_send(G_R1, c)

        def data_gradient(j):
            act[j] = dot(r1w[j], received(D_L1IN, j), 1, 0).astype(BF)

        each(c, data_gradient)
        pltpu.make_async_copy(act.at[rows(c)], ginp_h.at[rows(c)], load_sem.at[7 + c]).start()

    loop(NCH, step)
    def step(c):
        y_forward(R2_OUT, c)
        finish(G_L1, c)
        x_done(G_L1, c)
        x_sum(G_R1, c)

    loop(NCH, step)

    def step(c):
        arrived(R2_OUT, c)
        each(c, lambda j: gradient(G_L2, j, dot(received(R2_OUT, j), cot[j], 1, 1)))
        x_send(G_L2, c)

    loop(NCH, step)

    def step(c):
        x_sum(G_L2, c)
        finish(G_R1, c)

    loop(NCH, step)

    def step(c):
        finish(G_L2, c)
        sends_done(D_L1IN, c)
        sends_done(R2_OUT, c)
        x_done(G_R1, c)
        x_done(G_L2, c)
        pltpu.make_async_copy(act.at[rows(c)], ginp_h.at[rows(c)], load_sem.at[7 + c]).wait()
        for g in range(4):
            await_bytes(zout.at[g, rows(c)], ls.at[g, c])
            pltpu.make_async_copy(total.at[g, rows(c)], grads_h[g].at[rows(c)], out_sem.at[g, c]).wait()

    loop(NCH, step)


def body(inputs, hidden_pre, cotangent, r1_weight, l1_weight, r2_weight, l2_weight):
    anywhere = pl.BlockSpec(memory_space=pl.ANY)
    vmem, dma = pltpu.VMEM, pltpu.SemaphoreType.DMA
    grad = jax.ShapeDtypeStruct((NB, 32, B), F32)
    wide, square = (NB, B, T), (NB, B, B)
    return pl.pallas_call(
        kernel,
        name="monarch_backward",
        out_shape=(jax.ShapeDtypeStruct(wide, BF), grad, grad, grad, grad),
        in_specs=[anywhere] * 7,
        out_specs=(anywhere,) * 5,
        scratch_shapes=[
            vmem(wide, BF), vmem(wide, BF), vmem(wide, BF),
            vmem(square, BF), vmem(square, BF), vmem(square, BF), vmem(square, BF),
            vmem(wide, BF),
            vmem((2, 16, NB, NB, T), BF),
            vmem((4, 8, NB, NB, T), BF),
            vmem((4, NB, 16, NB, T), BF),
            vmem((2, NB, 2, 4, 32, B), BF),
            vmem((4, 3, NB, 2, 32, B), BF),
            vmem((4, NB, 32, B), BF),
            vmem((4, NB, 32, B), BF),
            vmem((4, NB, 32, B), F32),
            vmem((NB * B, LANES), F32),
            vmem((B, T), F32),
            dma((7 + NCH,)),
        ]
        + [dma((4, NCH))] * 10,
        compiler_params=pltpu.CompilerParams(
            collective_id=0, has_side_effects=True, vmem_limit_bytes=67_000_000
        ),
    )(inputs, hidden_pre, cotangent, r1_weight, l1_weight, r2_weight, l2_weight)


def solution(mesh):
    act_spec, weight = P("mp", None, "dp"), P("mp", None, None)
    return jax.shard_map(
        body,
        mesh=mesh,
        in_specs=(act_spec,) * 3 + (weight,) * 4,
        out_specs=(act_spec,) + (P("mp", "dp", None),) * 4,
        check_vma=False,
    )
```

time: 342 us -> 209 us (0.61)
  Pallas kernels: 0 us -> 201 us
  waiting for transfers between devices: 117 us -> 0 us
  blocking collectives: 111 us -> 0 us
  matrix products: 41.5 us -> 0 us
  local copies, waits for them, and re-layouts: 43.6 us -> 7.27 us
  between operations: 13.9 us -> 0.67 us
  starting transfers between devices: 8.35 us -> 0 us
  other arithmetic: 5.37 us -> 0 us
    pallas_call x0 -> x1, Pallas kernels: none -> 201 us  [body(): pl.pallas_call(kernel, name='monarch_backward', out_shape=(jax.ShapeDtype...]
    all_to_all x2 -> x0, blocking collectives: 111 us -> none  [the longest x1 62.6 us: body(): lax.all_to_all(d_l1in, 'mp', split_axis=1, concat_axis=0, tiled=True)]
    all_to_all x2 -> x0, waiting for transfers between devices: 89.9 us -> none  [the longest x1 47.1 us: body(): lax.all_to_all(d_l2in, 'mp', split_axis=1, concat_axis=0, tiled=True)]
    dot_general x10 -> x0, matrix products: 41.5 us -> none  [contract(): return jnp.einsum(form, left, right, preferred_element_type=jnp.float32)]
    reduce_scatter x4 -> x0, waiting for transfers between devices: 26.9 us -> none  [the longest x1 26.9 us: body(): lax.psum_scatter(term_r1.astype(jnp.bfloat16), 'dp', scatter_dimension=1,...]
    convert_element_type x5 -> x0, local copies, waits for them, and re-layouts: 20.6 us -> none  [the longest x1 5.09 us: body(): r2_out = contract('oqr,oqt->ort', r2_weight, act).astype(jnp.bfloat16)]
    unnamed x19 -> x13, local copies, waits for them, and re-layouts: 18.4 us -> 7.27 us
    all_to_all x2 -> x0, starting transfers between devices: 8.19 us -> none  [the longest x1 4.45 us: body(): lax.all_to_all(r1_out, 'mp', split_axis=1, concat_axis=0, tiled=True)]
  transfers between devices with their start and end apart: 6 -> 0, of which waited for: 3 -> 0; matrix products, arithmetic and copies ran while one was open for 18% -> 0% of each run, Pallas kernels for 0% -> 0%
where the time goes in v1:
time: 209 us
  Pallas kernels  201 us (96%)
  local copies, waits for them, and re-layouts  7.27 us (3%)
    pallas_call x1, Pallas kernels, body(): pl.pallas_call(kernel, name='monarch_backward', out_shape=(jax.ShapeDtype...  201 us
    unnamed x13, local copies, waits for them, and re-layouts  7.27 us

profile of v1, /device:TPU:0, one launch (start us, length us, event | category | flops | bytes accessed | tf_op | source)
XLA Modules:
  0.0 209.1 jit_solution(16792643428106345377)
XLA Ops:
  0.6 201.1 %monarch_backward.1 = (bf16[16,256,384]{2,1,0:T(8,128)(2,1)}, f32[16,32,256]{2,1,0:T(8,128)}, f32[16,32,256]{2,1,0:T(8,128)}, f32[16,32,256]{2,1,0:T(8,128)}, f32[16,32,256]{2,1,0:T(8,128)}) custom-call(bf16[16,256,384]{2,1,0:T(8,128)(2,1)} %inp_h.1, bf16[16,256,384]{2,1,0:T(8,128)(2,1)} %hid_h.1, bf16[16,256,384]{2,1,0:T(8,128)(2,1)} %cot_h.1, ...), custom_call_target="tpu_custom_call" | custom-call | tf_op jit(solution)/shard_map/monarch_backward/pallas_call | solution.py:299
  201.8 0.0 copy-start.3
  201.8 0.0 copy-start.2
  201.8 0.0 copy-start.1
  201.8 4.1 %copy.17 = bf16[16,256,384]{2,1,0:T(8,128)(2,1)} copy(bf16[16,256,384]{2,1,0:T(8,128)(2,1)} %get-tuple-element.10) | data formatting | bytes 6291456
  205.9 0.0 copy-done.3
  205.9 0.0 copy-start
  205.9 0.8 copy.18
  206.7 0.0 copy-done.2
  206.7 0.8 copy.19
  207.5 0.0 copy-done.1
  207.5 0.8 copy.20
  208.3 0.0 copy-done
  208.3 0.8 copy.21
Async XLA Ops:
  201.8 4.1 %copy-start.3 = (f32[16,32,256]{2,1,0:T(8,128)S(1)}, f32[16,32,256]{2,1,0:T(8,128)}, u32[]{:S(2)}) copy-start(f32[16,32,256]{2,1,0:T(8,128)} %get-tuple-element.11) | copy-start | bytes 1572868
  201.8 4.9 %copy-start.2 = (f32[16,32,256]{2,1,0:T(8,128)S(1)}, f32[16,32,256]{2,1,0:T(8,128)}, u32[]{:S(2)}) copy-start(f32[16,32,256]{2,1,0:T(8,128)} %get-tuple-element.12) | copy-start | bytes 1572868
  201.8 5.7 %copy-start.1 = (f32[16,32,256]{2,1,0:T(8,128)S(1)}, f32[16,32,256]{2,1,0:T(8,128)}, u32[]{:S(2)}) copy-start(f32[16,32,256]{2,1,0:T(8,128)} %get-tuple-element.13) | copy-start | bytes 1572868
  205.9 2.4 %copy-start = (f32[16,32,256]{2,1,0:T(8,128)S(1)}, f32[16,32,256]{2,1,0:T(8,128)}, u32[]{:S(2)}) copy-start(f32[16,32,256]{2,1,0:T(8,128)} %get-tuple-element.14) | copy-start | bytes 1572868

commit v2 on v1

v2 whole, which is shorter than its diff:
```python
import jax
import jax.numpy as jnp
from jax import lax
from jax.experimental import pallas as pl
from jax.experimental.pallas import tpu as pltpu
from jax.sharding import PartitionSpec as P

BF = jnp.bfloat16
F32 = jnp.float32
MESH = pl.DeviceIdType.MESH
NB, B, T = 16, 256, 384
LANES = 128
COEFF = 0.7978845608
D_L2IN, D_L1IN, R1_OUT, R2_OUT = range(4)
G_R2, G_R1, G_L1, G_L2 = range(4)
LANE_CHUNKS = (True, True, False, False)
CHUNKS = (3, 3, 4, 8)
SLOT = (0, 1, 2, 0)
SUMS = (4, 4, 4, 8)


def dot(left, right, l_dim, r_dim):
    return lax.dot_general(
        left, right, (((l_dim,), (r_dim,)), ((), ())), preferred_element_type=F32
    )


def loop(count, step, unroll=1):
    lax.fori_loop(0, count, lambda i, carry: (step(i), carry)[1], 0, unroll=4 if count == NB else unroll)


def kernel(
    inp_h, hid_h, cot_h, r1_h, l1_h, r2_h, l2_h,
    ginp_h, gr1_h, gl1_h, gr2_h, gl2_h,
    inp, hid, cot, r1w, r2w, l_w,
    act, send, arrive, recv, part, xin, zout, zin, total, stage,
    load_sem, out_sem, zs, zr, yo, yf, yr, xs, xr, ls, lr,
):
    d, m = lax.axis_index("dp"), lax.axis_index("mp")
    x, zl = d % 4, d // 4
    zh, yc = m // 8, m % 8
    y, core = yc // 2, yc % 2
    z_mate = (d, (1 - zh) * 8 + yc)
    l_mate = ((1 - zl) * 4 + x, m)
    near = []
    for dy, dc in ((2, 0), (2, 1), (1, 0), (3, 0), (1, 1), (3, 1), (0, 1)):
        near.append(((y + dy) % 4) * 2 + (core + dc) % 2)
    x_mates = [(zl * 4 + (x + dx) % 4, m) for dx in (1, 2, 3)]
    mate_m = (1 - zh) * 8 + yc

    def load(i, src, dst):
        return pltpu.make_async_copy(src, dst, load_sem.at[i])

    def cot_part(tc):
        span = pl.ds(tc * LANES, LANES)
        return load(tc, cot_h.at[:, :, span], cot.at[:, :, span])

    first = [load(3, l2_h, l_w), cot_part(0), cot_part(1), cot_part(2)]
    later = [
        load(i + 4, src, dst)
        for i, (src, dst) in enumerate(((r1_h, r1w), (inp_h, inp), (hid_h, hid), (r2_h, r2w)))
    ]
    last = load(8, l1_h, l_w)
    for copy in first:
        copy.start()

    barrier = pltpu.get_barrier_semaphore()
    mates = [z_mate, l_mate] + [(d, zh * 8 + n) for n in near] + x_mates
    for mate in mates:
        pl.semaphore_signal(barrier, inc=1, device_id=mate, device_id_type=MESH)

    def rows(k, c):
        if LANE_CHUNKS[k]:
            return pl.ds(0, NB)
        return pl.ds(c * (NB // CHUNKS[k]), NB // CHUNKS[k])

    def lanes(k, c):
        if LANE_CHUNKS[k]:
            return pl.ds(pl.multiple_of(c * LANES, LANES), LANES)
        return pl.ds(0, T)

    def remote(src, dst, s_sem, r_sem, device):
        return pltpu.make_async_remote_copy(
            src_ref=src, dst_ref=dst, send_sem=s_sem, recv_sem=r_sem, device_id=device, device_id_type=MESH
        )

    def await_bytes(ref, sem):
        pltpu.make_async_copy(ref, ref, sem).wait()

    def z_send(k, c):
        remote(
            send.at[SLOT[k], pl.ds((1 - zh) * 8, 8), rows(k, c), :, lanes(k, c)],
            arrive.at[k, :, rows(k, c), :, lanes(k, c)],
            zs.at[k, c], zr.at[k, c], z_mate,
        ).start()

    def y_own(k, c):
        here = recv.at[k, rows(k, c), m, :, lanes(k, c)]
        for n in near:
            remote(
                send.at[SLOT[k], zh * 8 + n, rows(k, c), :, lanes(k, c)], here,
                yo.at[k, c], yr.at[k, c], (d, zh * 8 + n),
            ).start()
        pltpu.make_async_copy(
            send.at[SLOT[k], m, rows(k, c), :, lanes(k, c)], here, yr.at[k, c]
        ).start()

    def dispatch(k, c):
        z_send(k, c)
        y_own(k, c)

    def forward(k, c):
        await_bytes(arrive.at[k, :, rows(k, c), :, lanes(k, c)], zr.at[k, c])
        here = recv.at[k, rows(k, c), mate_m, :, lanes(k, c)]
        for n in near:
            remote(
                arrive.at[k, n, rows(k, c), :, lanes(k, c)], here,
                yf.at[k, c], yr.at[k, c], (d, zh * 8 + n),
            ).start()
        pltpu.make_async_copy(arrive.at[k, yc, rows(k, c), :, lanes(k, c)], here, yr.at[k, c]).start()

    def arrived(k, c):
        await_bytes(recv.at[k, rows(k, c), :, :, lanes(k, c)], yr.at[k, c])

    def sends_done(k):
        def step(c):
            seven = arrive.at[k, pl.ds(0, 7), rows(k, c), :, lanes(k, c)]
            await_bytes(arrive.at[k, :, rows(k, c), :, lanes(k, c)], zs.at[k, c])
            await_bytes(seven, yo.at[k, c])
            await_bytes(seven, yf.at[k, c])

        loop(CHUNKS[k], step)

    def produce(k, tc, weight, w_dim, data):
        span = pl.ds(pl.multiple_of(tc * LANES, LANES), LANES)

        def block(j):
            stage[pl.ds(j, B, stride=NB), :] = dot(weight[j], data[j, :, span], w_dim, 0)

        def pack(dest):
            rows_of = pl.ds(pl.multiple_of(dest * B, B), B)
            send[SLOT[k], dest, :, :, span] = stage[rows_of, :].astype(BF).reshape(NB, NB, LANES)

        loop(NB, block)
        loop(NB, pack)

    def received(k, j):
        return recv[k, j].reshape(B, T)

    def piece(g, c):
        return pl.ds(c * (NB // SUMS[g]), NB // SUMS[g])

    def each(g, c, step):
        loop(NB // SUMS[g], lambda i: step(c * (NB // SUMS[g]) + i), NB // SUMS[g])

    def gradient(g, c, product):
        def block(j):
            part[g % 2, j] = product(j).astype(BF).reshape(2, 4, 32, B)

        each(g, c, block)
        for i, mate in enumerate(x_mates):
            remote(
                part.at[g % 2, piece(g, c), :, (x + i + 1) % 4], xin.at[g, i, piece(g, c)],
                xs.at[g, c], xr.at[g, c], mate,
            ).start()

    def x_done(g):
        loop(SUMS[g], lambda c: await_bytes(xin.at[g, :, piece(g, c)], xs.at[g, c]))

    def x_sum(g, c):
        await_bytes(xin.at[g, :, piece(g, c)], xr.at[g, c])

        def block(j):
            def joined(half):
                value = part[g % 2, j, half, x].astype(F32)
                for s in range(3):
                    value += xin[g, s, j, half].astype(F32)
                return value

            zout[g, j] = joined(1 - zl).astype(BF)
            total[g, j] = joined(zl)

        each(g, c, block)
        remote(zout.at[g, piece(g, c)], zin.at[g, piece(g, c)], ls.at[g, c], lr.at[g, c], l_mate).start()

    grads_h = {G_R2: gr2_h, G_L1: gl1_h, G_R1: gr1_h, G_L2: gl2_h}

    def out_copy(g, c):
        return pltpu.make_async_copy(total.at[g, piece(g, c)], grads_h[g].at[piece(g, c)], out_sem.at[g, c])

    def finish(g, c):
        await_bytes(zin.at[g, piece(g, c)], lr.at[g, c])

        def block(j):
            total[g, j] += zin[g, j].astype(F32)

        each(g, c, block)
        out_copy(g, c).start()

    def gelu_parts(v):
        return v, jnp.tanh(COEFF * (v + 0.044715 * v * v * v))

    def gelu_block(j):
        def group(i):
            span = pl.ds(pl.multiple_of(i * 32, 32), 32)
            v, t = gelu_parts(hid[j, span, :].astype(F32))
            act[j, span, :] = (0.5 * v * (1.0 + t)).astype(BF)

        loop(B // 32, group)

    def d_hidden(tc):
        span = pl.ds(pl.multiple_of(tc * LANES, LANES), LANES)

        def block(j):
            v, t = gelu_parts(hid[j, :, span].astype(F32))
            slope = 0.5 * (1.0 + t) + 0.5 * v * (1.0 - t * t) * COEFF * (1.0 + 3.0 * 0.044715 * v * v)
            back = dot(r2w[j], recv[D_L2IN, j, :, :, span].reshape(B, LANES), 1, 0)
            hid[j, :, span] = (back * slope).astype(BF)

        loop(NB, block)

    def grad_r2(c):
        gradient(G_R2, c, lambda j: dot(act[j], received(D_L2IN, j), 1, 1))

    def grad_r1(c):
        gradient(G_R1, c, lambda j: dot(inp[j], received(D_L1IN, j), 1, 1))

    def grad_l1(c):
        gradient(G_L1, c, lambda j: dot(received(R1_OUT, j), hid[j], 1, 1))

    def grad_l2(c):
        gradient(G_L2, c, lambda j: dot(received(R2_OUT, j), cot[j], 1, 1))

    def out_inputs(c):
        return pltpu.make_async_copy(act.at[pl.ds(c * 4, 4)], ginp_h.at[pl.ds(c * 4, 4)], load_sem.at[9 + c])

    def grad_inputs(c):
        def block(i):
            act[c * 4 + i] = dot(r1w[c * 4 + i], received(D_L1IN, c * 4 + i), 1, 0).astype(BF)

        loop(4, block, 4)
        out_inputs(c).start()

    for tc in range(3):
        if tc == 0:
            first[0].wait()
        first[1 + tc].wait()
        if tc == 1:
            for copy in later:
                copy.start()
        produce(D_L2IN, tc, l_w, 1, cot)
        if tc == 0:
            pl.semaphore_wait(barrier, len(mates))
        dispatch(D_L2IN, tc)
    last.start()
    later[0].wait()
    later[1].wait()
    loop(3, lambda tc: produce(R1_OUT, tc, r1w, 0, inp))
    later[2].wait()
    loop(NB, gelu_block)
    later[3].wait()
    last.wait()

    forward(D_L2IN, 0)

    def step(c):
        arrived(D_L2IN, c)
        d_hidden(c)
        produce(D_L1IN, c, l_w, 1, hid)
        dispatch(D_L1IN, c)

    def follow(c):
        step(c)
        forward(D_L2IN, c + 1)

    loop(2, follow)
    step(2)
    forward(D_L1IN, 0)
    loop(4, grad_r2)
    sends_done(D_L2IN)
    loop(3, lambda tc: produce(R2_OUT, tc, r2w, 0, act))
    forward(D_L1IN, 1)
    dispatch(R1_OUT, 0)
    dispatch(R1_OUT, 1)
    x_sum(G_R2, 0)
    x_sum(G_R2, 1)
    forward(D_L1IN, 2)
    dispatch(R1_OUT, 2)
    dispatch(R1_OUT, 3)
    x_sum(G_R2, 2)
    x_sum(G_R2, 3)
    loop(8, lambda c: z_send(R2_OUT, c))
    loop(3, lambda c: arrived(D_L1IN, c))
    x_done(G_R2)
    loop(4, grad_r1)
    forward(R1_OUT, 0)
    loop(4, grad_inputs)
    forward(R1_OUT, 1)
    y_own(R2_OUT, 0)
    y_own(R2_OUT, 1)
    x_sum(G_R1, 0)
    x_sum(G_R1, 1)
    arrived(R1_OUT, 0)
    grad_l1(0)
    forward(R1_OUT, 2)
    y_own(R2_OUT, 2)
    y_own(R2_OUT, 3)
    x_sum(G_R1, 2)
    x_sum(G_R1, 3)
    arrived(R1_OUT, 1)
    grad_l1(1)
    forward(R1_OUT, 3)
    y_own(R2_OUT, 4)
    x_done(G_R1)
    arrived(R1_OUT, 2)
    grad_l1(2)
    x_sum(G_L1, 0)
    forward(R2_OUT, 0)
    y_own(R2_OUT, 5)
    arrived(R1_OUT, 3)
    grad_l1(3)
    x_sum(G_L1, 1)

    forward(R2_OUT, 1)
    y_own(R2_OUT, 6)
    arrived(R2_OUT, 0)
    grad_l2(0)
    x_sum(G_L1, 2)
    forward(R2_OUT, 2)
    y_own(R2_OUT, 7)
    arrived(R2_OUT, 1)
    grad_l2(1)
    x_sum(G_L1, 3)

    def step(c):
        forward(R2_OUT, c)
        arrived(R2_OUT, c - 1)
        grad_l2(c - 1)
        x_sum(G_L2, c - 3)

    lax.fori_loop(3, 8, lambda c, carry: (step(c), carry)[1], 0)
    x_sum(G_L2, 5)
    arrived(R2_OUT, 7)
    grad_l2(7)
    loop(4, lambda c: finish(G_R2, c))
    x_sum(G_L2, 6)
    x_sum(G_L2, 7)
    for g in (G_R1, G_L1, G_L2):
        loop(SUMS[g], lambda c, g=g: finish(g, c))

    for k in (D_L1IN, R1_OUT, R2_OUT):
        sends_done(k)
    x_done(G_L1)
    x_done(G_L2)
    loop(4, lambda c: out_inputs(c).wait())
    for g in range(4):

        def step(c, g=g):
            await_bytes(zout.at[g, piece(g, c)], ls.at[g, c])
            out_copy(g, c).wait()

        loop(SUMS[g], step)


def deliver(*refs):
    srcs, outs, bufs, (s_in, s_out) = refs[:5], refs[5:10], refs[10:15], refs[15:]
    parts = [(0, pl.ds(c * 4, 4)) for c in range(4)] + [(i, pl.ds(0, NB)) for i in range(1, 5)]
    reads = [
        pltpu.make_async_copy(srcs[i].at[p], bufs[i].at[p], s_in.at[n]) for n, (i, p) in enumerate(parts)
    ]
    writes = [
        pltpu.make_async_copy(bufs[i].at[p], outs[i].at[p], s_out.at[n]) for n, (i, p) in enumerate(parts)
    ]
    for read in reads:
        read.start()
    for read, write in zip(reads, writes):
        read.wait()
        write.start()
    for write in writes:
        write.wait()


def body(inputs, hidden_pre, cotangent, r1_weight, l1_weight, r2_weight, l2_weight):
    anywhere = pl.BlockSpec(memory_space=pl.ANY)
    vmem, dma = pltpu.VMEM, pltpu.SemaphoreType.DMA
    grad = jax.ShapeDtypeStruct((NB, 32, B), F32)
    wide, square = (NB, B, T), (NB, B, B)
    results = pl.pallas_call(
        kernel,
        name="monarch_backward",
        out_shape=(jax.ShapeDtypeStruct(wide, BF), grad, grad, grad, grad),
        in_specs=[anywhere] * 7,
        out_specs=(anywhere,) * 5,
        scratch_shapes=[
            vmem(wide, BF), vmem(wide, BF), vmem(wide, BF),
            vmem(square, BF), vmem(square, BF), vmem(square, BF),
            vmem(wide, BF),
            vmem((3, 16, NB, NB, T), BF),
            vmem((4, 8, NB, NB, T), BF),
            vmem((4, NB, 16, NB, T), BF),
            vmem((2, NB, 2, 4, 32, B), BF),
            vmem((4, 3, NB, 2, 32, B), BF),
            vmem((4, NB, 32, B), BF),
            vmem((4, NB, 32, B), BF),
            vmem((4, NB, 32, B), F32),
            vmem((NB * B, LANES), F32),
            dma((13,)),
        ]
        + [dma((4, 8))] * 10,
        compiler_params=pltpu.CompilerParams(
            collective_id=0, has_side_effects=True, vmem_limit_bytes=67_000_000
        ),
    )(inputs, hidden_pre, cotangent, r1_weight, l1_weight, r2_weight, l2_weight)
    shapes = tuple(jax.ShapeDtypeStruct(r.shape, r.dtype) for r in results)
    return pl.pallas_call(
        deliver,
        name="deliver",
        out_shape=shapes,
        in_specs=[anywhere] * 5,
        out_specs=(anywhere,) * 5,
        scratch_shapes=[vmem(r.shape, r.dtype) for r in results] + [dma((8,)), dma((8,))],
        compiler_params=pltpu.CompilerParams(vmem_limit_bytes=67_000_000),
    )(*results)


def solution(mesh):
    act_spec, weight = P("mp", None, "dp"), P("mp", None, None)
    return jax.shard_map(
        body,
        mesh=mesh,
        in_specs=(act_spec,) * 3 + (weight,) * 4,
        out_specs=(act_spec,) + (P("mp", "dp", None),) * 4,
        check_vma=False,
    )
```

time: 209 us -> 185 us (0.89)
  Pallas kernels: 201 us -> 184 us
  local copies, waits for them, and re-layouts: 7.27 us -> 0 us
    pallas_call x1, Pallas kernels: 201 us -> 180 us  [body(): pl.pallas_call(kernel, name='monarch_backward', out_shape=(jax.ShapeDtype...]
    unnamed x13 -> x0, local copies, waits for them, and re-layouts: 7.27 us -> none
    pallas_call x0 -> x1, Pallas kernels: none -> 4.46 us  [body(): pl.pallas_call(deliver, name='deliver', out_shape=shapes, in_specs=[anywh...]
where the time goes in v2:
time: 185 us
  Pallas kernels  184 us (99%)
    pallas_call x1, Pallas kernels, body(): pl.pallas_call(kernel, name='monarch_backward', out_shape=(jax.ShapeDtype...  180 us
    pallas_call x1, Pallas kernels, body(): pl.pallas_call(deliver, name='deliver', out_shape=shapes, in_specs=[anywh...  4.46 us

profile of v2, /device:TPU:0, one launch (start us, length us, event | category | flops | bytes accessed | tf_op | source)
XLA Modules:
  0.0 185.1 jit_solution(14058755250806832416)
XLA Ops:
  0.6 180.0 %monarch_backward.1 = (bf16[16,256,384]{2,1,0:T(8,128)(2,1)}, f32[16,32,256]{2,1,0:T(8,128)}, f32[16,32,256]{2,1,0:T(8,128)}, f32[16,32,256]{2,1,0:T(8,128)}, f32[16,32,256]{2,1,0:T(8,128)}) custom-call(bf16[16,256,384]{2,1,0:T(8,128)(2,1)} %inp_h.1, bf16[16,256,384]{2,1,0:T(8,128)(2,1)} %hid_h.1, bf16[16,256,384]{2,1,0:T(8,128)(2,1)} %cot_h.1, ...), custom_call_target="tpu_custom_call" | custom-call | tf_op jit(solution)/shard_map/monarch_backward/pallas_call | solution.py:388
  180.6 4.5 %deliver.1 = (bf16[16,256,384]{2,1,0:T(8,128)(2,1)}, f32[16,32,256]{2,1,0:T(8,128)}, f32[16,32,256]{2,1,0:T(8,128)}, f32[16,32,256]{2,1,0:T(8,128)}, f32[16,32,256]{2,1,0:T(8,128)}) custom-call(bf16[16,256,384]{2,1,0:T(8,128)(2,1)} %get-tuple-element.10.refs_0_, f32[16,32,256]{2,1,0:T(8,128)} %get-tuple-element.11.refs_1_, ...), custom_call_target="tpu_custom_call" | custom-call | tf_op jit(solution)/shard_map/deliver/pallas_call | solution.py:415

commit v3 on v2

--- a/solution.py
+++ b/solution.py
@@ -262,6 +262,7 @@
     last.wait()
 
     forward(D_L2IN, 0)
+    y_own(R1_OUT, 0)
 
     def step(c):
         arrived(D_L2IN, c)
@@ -272,6 +273,7 @@
     def follow(c):
         step(c)
         forward(D_L2IN, c + 1)
+        y_own(R1_OUT, c + 1)
 
     loop(2, follow)
     step(2)
@@ -280,12 +282,12 @@
     sends_done(D_L2IN)
     loop(3, lambda tc: produce(R2_OUT, tc, r2w, 0, act))
     forward(D_L1IN, 1)
-    dispatch(R1_OUT, 0)
-    dispatch(R1_OUT, 1)
+    z_send(R1_OUT, 0)
+    z_send(R1_OUT, 1)
     x_sum(G_R2, 0)
     x_sum(G_R2, 1)
     forward(D_L1IN, 2)
-    dispatch(R1_OUT, 2)
+    z_send(R1_OUT, 2)
     dispatch(R1_OUT, 3)
     x_sum(G_R2, 2)
     x_sum(G_R2, 3)

time: 185 us -> 182 us (0.984)
  Pallas kernels: 184 us -> 180 us
    pallas_call x1, Pallas kernels: 180 us -> 176 us  [body(): pl.pallas_call(kernel, name='monarch_backward', out_shape=(jax.ShapeDtype...]
where the time goes in v3:
time: 182 us; the launch traced here: 181 us
  Pallas kernels  180 us (99%)
    pallas_call x1, Pallas kernels, body(): pl.pallas_call(kernel, name='monarch_backward', out_shape=(jax.ShapeDtype...  176 us
    pallas_call x1, Pallas kernels, body(): pl.pallas_call(deliver, name='deliver', out_shape=shapes, in_specs=[anywh...  4.46 us

profile of v3, /device:TPU:0, one launch (start us, length us, event | category | flops | bytes accessed | tf_op | source)
XLA Modules:
  0.0 180.9 jit_solution(4882076698226866549)
XLA Ops:
  0.6 175.8 %monarch_backward.1 = (bf16[16,256,384]{2,1,0:T(8,128)(2,1)}, f32[16,32,256]{2,1,0:T(8,128)}, f32[16,32,256]{2,1,0:T(8,128)}, f32[16,32,256]{2,1,0:T(8,128)}, f32[16,32,256]{2,1,0:T(8,128)}) custom-call(bf16[16,256,384]{2,1,0:T(8,128)(2,1)} %inp_h.1, bf16[16,256,384]{2,1,0:T(8,128)(2,1)} %hid_h.1, bf16[16,256,384]{2,1,0:T(8,128)(2,1)} %cot_h.1, ...), custom_call_target="tpu_custom_call" | custom-call | tf_op jit(solution)/shard_map/monarch_backward/pallas_call | solution.py:390
  176.5 4.5 %deliver.1 = (bf16[16,256,384]{2,1,0:T(8,128)(2,1)}, f32[16,32,256]{2,1,0:T(8,128)}, f32[16,32,256]{2,1,0:T(8,128)}, f32[16,32,256]{2,1,0:T(8,128)}, f32[16,32,256]{2,1,0:T(8,128)}) custom-call(bf16[16,256,384]{2,1,0:T(8,128)(2,1)} %get-tuple-element.10.refs_0_, f32[16,32,256]{2,1,0:T(8,128)} %get-tuple-element.11.refs_1_, ...), custom_call_target="tpu_custom_call" | custom-call | tf_op jit(solution)/shard_map/deliver/pallas_call | solution.py:417
